TPU v7x, 32 devices: a whole 2x2x4 slice. The times are simulated.
32 devices in a mesh: ctx: 16 (over z, y, core), ch: 2 (over x).
Axes of the slice: x: 2, y: 2, z: 4, core: 2. Of those that a mesh axis runs over, the one named last changes fastest.
Arguments:
- inputs: float32 [12288, 2048], P('ctx', 'ch'), may hold values from -6 to 6
- cotangent: float32 [12288, 2048], P('ctx', 'ch'), may hold values from -6 to 6
- filter_rows: float32 [1536, 2048], P('ctx', 'ch'), may hold values from -0.15625 to 0.15625
- skip_gain: float32 [2048], P('ch'), may hold values from -1 to 1
- band_blocks: int32 [2048], P('ch'), may hold values from 1 to 2
Outputs:
- outputs: float32 [12288, 2048], P('ctx', 'ch')
- input_grad: float32 [2048, 12288], P(('ch', 'ctx'))
All inputs are finite; a program needn't handle non-finite values.
Results may differ from a plain program's by a relative error of at most 0.00007.
Values sent between devices are 32-bit elements; how exact they have to be, the bound alone decides.
A program may use at most 192 MiB of HBM per device.

v0:
```python
import math
import jax
import jax.numpy as jnp
from jax import lax
from jax.sharding import PartitionSpec as P

PRECISE = lax.Precision.HIGHEST


def passed_along(value, axis, steps):
    count = lax.axis_size(axis)
    initial, last = (max(0, -steps), min(count, count - steps))
    return lax.ppermute(value, axis, [(source, source + steps) for source in range(initial, last)])


def factor_pair(length):
    leading = 1
    candidate = 1
    while candidate * candidate <= length:
        if length % candidate == 0:
            leading = candidate
        candidate += 1
    return (leading, length // leading)


def twiddle_table(row_count, col_count, period, direction):
    product = (
        jnp.arange(row_count, dtype=jnp.int32)[:, None]
        * jnp.arange(col_count, dtype=jnp.int32)[None, :]
        % period
    )
    angle_val = product.astype(jnp.float32) * (2.0 * math.pi / period)
    return (jnp.cos(angle_val), direction * jnp.sin(angle_val))


def forward_real(signal, factors):
    leading, trailing = factors
    length = leading * trailing
    kept = trailing // 2 + 1
    grid_view = signal.reshape(leading, trailing, signal.shape[-1])
    cos_first, sin_first = twiddle_table(leading, leading, leading, -1.0)
    section_real = jnp.einsum("kn,nmc->kmc", cos_first, grid_view, precision=PRECISE)
    section_imag = jnp.einsum("kn,nmc->kmc", sin_first, grid_view, precision=PRECISE)
    turn_real, turn_imag = twiddle_table(leading, trailing, length, -1.0)
    rot_real = section_real * turn_real[:, :, None] - section_imag * turn_imag[:, :, None]
    rot_imag = section_real * turn_imag[:, :, None] + section_imag * turn_real[:, :, None]
    cos_second, sin_second = twiddle_table(trailing, kept, trailing, -1.0)
    out_real = jnp.einsum("kmc,mj->kjc", rot_real, cos_second, precision=PRECISE) - jnp.einsum(
        "kmc,mj->kjc", rot_imag, sin_second, precision=PRECISE
    )
    out_imag = jnp.einsum("kmc,mj->kjc", rot_real, sin_second, precision=PRECISE) + jnp.einsum(
        "kmc,mj->kjc", rot_imag, cos_second, precision=PRECISE
    )
    return jnp.stack([out_real, out_imag])


def inverse_real(spectrum, factors, channel_major):
    leading, trailing = factors
    length = leading * trailing
    kept = trailing // 2 + 1
    freq_index = (
        jnp.arange(leading, dtype=jnp.int32)[:, None]
        + leading * jnp.arange(kept, dtype=jnp.int32)[None, :]
    )
    edge_bin = (freq_index == 0) | (2 * freq_index == length)
    weights = jnp.where(edge_bin, 1.0, jnp.where(2 * freq_index < length, 2.0, 0.0)).astype(
        jnp.float32
    )
    spec_real = spectrum[0] * weights[:, :, None]
    spec_imag = spectrum[1] * weights[:, :, None]
    cos_second, sin_second = twiddle_table(kept, trailing, trailing, 1.0)
    part_real = jnp.einsum("kjc,jm->kmc", spec_real, cos_second, precision=PRECISE) - jnp.einsum(
        "kjc,jm->kmc", spec_imag, sin_second, precision=PRECISE
    )
    part_imag = jnp.einsum("kjc,jm->kmc", spec_real, sin_second, precision=PRECISE) + jnp.einsum(
        "kjc,jm->kmc", spec_imag, cos_second, precision=PRECISE
    )
    turn_real, turn_imag = twiddle_table(leading, trailing, length, 1.0)
    rot_real = part_real * turn_real[:, :, None] - part_imag * turn_imag[:, :, None]
    rot_imag = part_real * turn_imag[:, :, None] + part_imag * turn_real[:, :, None]
    cos_first, sin_first = twiddle_table(leading, leading, leading, 1.0)
    if channel_major:
        result = jnp.einsum("nk,kmc->cnm", cos_first, rot_real, precision=PRECISE) - jnp.einsum(
            "nk,kmc->cnm", sin_first, rot_imag, precision=PRECISE
        )
        return result.reshape(result.shape[0], length) / length
    result = jnp.einsum("nk,kmc->nmc", cos_first, rot_real, precision=PRECISE) - jnp.einsum(
        "nk,kmc->nmc", sin_first, rot_imag, precision=PRECISE
    )
    return result.reshape(length, result.shape[-1]) / length


def spectral_product(tap_spec, panel_spec, conjugate):
    tap_real, tap_imag = (tap_spec[0], tap_spec[1])
    if conjugate:
        tap_imag = -tap_imag
    panel_real, panel_imag = (panel_spec[0], panel_spec[1])
    return jnp.stack(
        [
            tap_real * panel_real - tap_imag * panel_imag,
            tap_real * panel_imag + tap_imag * panel_real,
        ]
    )


def local(inputs, cotangent, filter_rows, skip_gain, band_blocks):
    block_len = inputs.shape[0]
    factors = factor_pair(2 * block_len)
    piece_rows = lax.all_gather(filter_rows, "ctx", axis=0, tiled=True)
    lag_index = jnp.arange(piece_rows.shape[0], dtype=jnp.int32)
    keep_mask = lag_index[:, None] < band_blocks[None, :] * block_len
    filter_full = jnp.where(keep_mask, piece_rows, jnp.zeros_like(piece_rows))
    lag_zero = jnp.arange(filter_full.shape[0], dtype=jnp.int32)[:, None] == 0
    filter_full = filter_full + jnp.where(lag_zero, skip_gain[None, :], 0.0)
    blank_rows = jnp.zeros_like(inputs)
    lower_one = passed_along(inputs, "ctx", 1)
    upper_one = passed_along(cotangent, "ctx", -1)
    own_forward = forward_real(jnp.concatenate([lower_one, inputs], axis=0), factors)
    own_backward = forward_real(jnp.concatenate([cotangent, upper_one], axis=0), factors)
    forward_sources = [own_forward]
    backward_sources = [own_backward]
    lag_block = 1
    forward_sources.append(passed_along(own_forward, "ctx", lag_block))
    backward_sources.append(passed_along(own_backward, "ctx", -lag_block))

    def tile_terms(totals, lag_block):
        tap_block = lax.slice_in_dim(
            filter_full, lag_block * block_len, (lag_block + 1) * block_len, axis=0
        )
        tap_spec = forward_real(jnp.concatenate([tap_block, blank_rows], axis=0), factors)
        forward_panel = forward_sources[lag_block]
        backward_panel = backward_sources[lag_block]
        return (
            totals[0] + spectral_product(tap_spec, forward_panel, False),
            totals[1] + spectral_product(tap_spec, backward_panel, True),
        )

    totals = tile_terms((0.0, 0.0), 0)
    lag_block = 1
    totals = tile_terms(totals, lag_block)
    forward_time = inverse_real(totals[0], factors, False)
    outputs = lax.slice_in_dim(forward_time, block_len, 2 * block_len, axis=0)
    backward_time = inverse_real(totals[1], factors, True)
    local_grad = lax.slice_in_dim(backward_time, 0, block_len, axis=1)
    input_grad = lax.all_to_all(local_grad, "ctx", split_axis=0, concat_axis=1, tiled=True)
    return (outputs, input_grad)


def solution(mesh):
    return jax.shard_map(
        local,
        mesh=mesh,
        in_specs=(P("ctx", "ch"), P("ctx", "ch"), P("ctx", "ch"), P("ch"), P("ch")),
        out_specs=(P("ctx", "ch"), P(("ch", "ctx"), None)),
        check_vma=False,
    )
```

profile of v0, /device:TPU:0, one launch (start us, length us, event | category | flops | bytes accessed | tf_op | source)
XLA Modules:
  0.0 702.1 jit_solution(13089642921306606010)
XLA Ops:
  19.7 10.0 %fusion.44 = f32[32,48,1024]{2,0,1:T(8,128)} fusion(f32[32,48,1024]{2,1,0:T(8,128)S(1)} %bitcast.317), kind=kOutput, calls=%fused_computation.69 | convolution fusion | flops 603995136 | bytes 12582912 | tf_op jit(solution)/shard_map/kn,nmc->kmc/dot_general | solution.py:43
  29.7 10.1 %fusion.46 = f32[32,48,1024]{2,0,1:T(8,128)} fusion(f32[32,48,1024]{2,1,0:T(8,128)S(1)} %bitcast.318), kind=kOutput, calls=%fused_computation.71 | convolution fusion | flops 603994112 | bytes 12582912 | tf_op jit(solution)/shard_map/kn,nmc->kmc/dot_general | solution.py:42
  39.8 10.3 %fusion.22 = f32[32,48,1024]{2,0,1:T(8,128)} fusion(f32[32,48,1024]{2,1,0:T(8,128)S(1)} %bitcast.303), kind=kOutput, calls=%fused_computation.47 | convolution fusion | flops 603994112 | bytes 12582912 | tf_op jit(solution)/shard_map/kn,nmc->kmc/dot_general | solution.py:42
  50.1 53.3 %all-gather.2.cloned.1.call-done = f32[1536,1024]{1,0:T(8,128)} async-done(((f32[96,1024]{1,0:T(8,128)}), f32[1536,1024]{1,0:T(8,128)}) %all-gather.2.cloned.1.call-update) | async-done | bytes 6291472 | tf_op jit(solution)/shard_map/all_gather | solution.py:109
  108.7 10.1 %fusion.32 = f32[32,48,1024]{2,0,1:T(8,128)} fusion(f32[32,48,1024]{2,1,0:T(8,128)S(1)} %bitcast.315), kind=kOutput, calls=%fused_computation.57 | convolution fusion | flops 603995136 | bytes 12582912 | tf_op jit(solution)/shard_map/kn,nmc->kmc/dot_general | solution.py:43
  118.7 10.4 %fusion.34 = f32[32,48,1024]{2,0,1:T(8,128)} fusion(f32[32,48,1024]{2,1,0:T(8,128)S(1)} %bitcast.316), kind=kOutput, calls=%fused_computation.59 | convolution fusion | flops 603994112 | bytes 12582912 | tf_op jit(solution)/shard_map/kn,nmc->kmc/dot_general | solution.py:42
  129.2 10.1 %fusion.56 = f32[32,48,1024]{2,0,1:T(8,128)} fusion(f32[32,48,1024]{2,1,0:T(8,128)S(1)} %bitcast.313), kind=kOutput, calls=%fused_computation.81 | convolution fusion | flops 603995136 | bytes 12582912 | tf_op jit(solution)/shard_map/kn,nmc->kmc/dot_general | solution.py:43
  139.2 10.3 %fusion.58 = f32[32,48,1024]{2,0,1:T(8,128)} fusion(f32[32,48,1024]{2,1,0:T(8,128)S(1)} %bitcast.314), kind=kOutput, calls=%fused_computation.83 | convolution fusion | flops 603994112 | bytes 12582912 | tf_op jit(solution)/shard_map/kn,nmc->kmc/dot_general | solution.py:42
  149.5 40.5 %multiply_subtract_fusion = (f32[32,48,1024]{2,0,1:T(8,128)}, f32[32,48,1024]{2,0,1:T(8,128)}, f32[32,48,1024]{2,0,1:T(8,128)}, f32[32,48,1024]{2,0,1:T(8,128)},...) fusion(f32[32,48,1024]{2,0,1:T(8,128)} %fusion.22, ...), kind=kOutput, calls=%fused_computation.28 | convolution fusion | flops 641743872 | bytes 100675584 | tf_op jit(solution)/shard_map/kn,nmc->kmc/dot_general | solution.py:43
  190.1 10.7 %fusion.12 = f32[25,32,1024]{2,0,1:T(8,128)S(1)} fusion(f32[32,48,1024]{2,0,1:T(8,128)} %get-tuple-element.13), kind=kOutput, calls=%fused_computation.37 | convolution fusion | flops 471870016 | bytes 9568256 | tf_op jit(solution)/shard_map/kmc,mj->kjc/dot_general | solution.py:51
  200.8 8.2 %fusion.14 = f32[25,32,1024]{2,0,1:T(8,128)} fusion(f32[32,48,1024]{2,0,1:T(8,128)S(1)} %copy-done.1), kind=kOutput, calls=%fused_computation.39 | convolution fusion | flops 471871200 | bytes 9568256 | tf_op jit(solution)/shard_map/kmc,mj->kjc/dot_general | solution.py:48
  209.1 8.6 %fusion.38 = f32[25,32,1024]{2,0,1:T(8,128)} fusion(f32[32,48,1024]{2,0,1:T(8,128)S(1)} %bitcast.306), kind=kOutput, calls=%fused_computation.63 | convolution fusion | flops 471871200 | bytes 9568256 | tf_op jit(solution)/shard_map/kmc,mj->kjc/dot_general | solution.py:48
  225.8 8.4 %fusion.136 = f32[25,32,1024]{2,0,1:T(8,128)S(1)} fusion(f32[25,32,1024]{2,0,1:T(8,128)S(1)} %fusion.12, f32[32,48,1024]{2,0,1:T(8,128)S(1)} %bitcast.298), kind=kOutput, calls=%fused_computation.157 | convolution fusion | flops 472690400 | bytes 12845056 | tf_op jit(solution)/shard_map/kmc,mj->kjc/dot_general | solution.py:51
  234.2 8.1 %fusion.133 = f32[25,32,1024]{2,0,1:T(8,128)S(1)} fusion(f32[25,32,1024]{2,0,1:T(8,128)S(1)} %copy-done.6, f32[32,48,1024]{2,0,1:T(8,128)S(1)} %bitcast.298), kind=kOutput, calls=%fused_computation.156 | convolution fusion | flops 472689216 | bytes 12845056 | tf_op jit(solution)/shard_map/kmc,mj->kjc/dot_general | solution.py:48
  247.0 10.3 %copy.136 = f32[2,32,25,1024]{3,1,2,0:T(8,128)} copy(f32[2,32,25,1024]{3,2,1,0:T(8,128)} %pad_maximum_fusion.1) | data formatting | bytes 13107200 | tf_op jit(solution)/shard_map/stack | solution.py:54
  258.6 8.1 %fusion.121 = f32[25,32,1024]{2,0,1:T(8,128)S(1)} fusion(f32[25,32,1024]{2,0,1:T(8,128)S(1)} %copy-done.5, f32[32,48,1024]{2,0,1:T(8,128)S(1)} %bitcast.296), kind=kOutput, calls=%fused_computation.152 | convolution fusion | flops 472689216 | bytes 12845056 | tf_op jit(solution)/shard_map/kmc,mj->kjc/dot_general | solution.py:48
  266.7 8.8 %fusion.124 = f32[25,32,1024]{2,0,1:T(8,128)} fusion(f32[25,32,1024]{2,0,1:T(8,128)S(1)} %fusion.36, f32[32,48,1024]{2,0,1:T(8,128)S(1)} %bitcast.296), kind=kOutput, calls=%fused_computation.153 | convolution fusion | flops 472690400 | bytes 12845056 | tf_op jit(solution)/shard_map/kmc,mj->kjc/dot_general | solution.py:51
  282.6 9.9 %copy.120 = f32[2,32,25,1024]{3,1,2,0:T(8,128)} copy(f32[2,32,25,1024]{3,2,1,0:T(8,128)} %pad_maximum_fusion) | data formatting | bytes 13107200 | tf_op jit(solution)/shard_map/stack | solution.py:54
  292.5 36.6 %collective-permute-start.1 = (f32[2,32,25,1024]{3,1,2,0:T(8,128)}, f32[2,32,25,1024]{3,1,2,0:T(8,128)}, u32[]{:S(2)}, u32[]{:S(2)}) collective-permute-start(f32[2,32,25,1024]{3,1,2,0:T(8,128)} %copy.120), channel_id=1, source_target_pairs={{0,2},{2,4},{4,6},{6,8},{8,10},{10,12},{12,14},{14,16},{16,18},{18... | collective-permute-start | bytes 19660808 | tf_op jit(solution)/shard_map/ppermute | solution.py:13
  329.3 8.1 %fusion.48 = f32[25,32,1024]{2,0,1:T(8,128)S(1)} fusion(f32[32,48,1024]{2,0,1:T(8,128)S(1)} %bitcast.302), kind=kOutput, calls=%fused_computation.73 | convolution fusion | flops 471870016 | bytes 9568256 | tf_op jit(solution)/shard_map/kmc,mj->kjc/dot_general | solution.py:51
  337.3 8.5 %fusion.50 = f32[25,32,1024]{2,0,1:T(8,128)} fusion(f32[32,48,1024]{2,0,1:T(8,128)S(1)} %bitcast.302), kind=kOutput, calls=%fused_computation.75 | convolution fusion | flops 471871200 | bytes 9568256 | tf_op jit(solution)/shard_map/kmc,mj->kjc/dot_general | solution.py:48
  345.8 8.1 %fusion.24 = f32[25,32,1024]{2,0,1:T(8,128)S(1)} fusion(f32[32,48,1024]{2,0,1:T(8,128)S(1)} %bitcast.300), kind=kOutput, calls=%fused_computation.49 | convolution fusion | flops 471870016 | bytes 9568256 | tf_op jit(solution)/shard_map/kmc,mj->kjc/dot_general | solution.py:51
  353.9 8.5 %fusion.26 = f32[25,32,1024]{2,0,1:T(8,128)} fusion(f32[32,48,1024]{2,0,1:T(8,128)S(1)} %bitcast.300), kind=kOutput, calls=%fused_computation.51 | convolution fusion | flops 471871200 | bytes 9568256 | tf_op jit(solution)/shard_map/kmc,mj->kjc/dot_general | solution.py:48
  362.3 8.4 %fusion.118 = f32[25,32,1024]{2,0,1:T(8,128)} fusion(f32[25,32,1024]{2,0,1:T(8,128)S(1)} %fusion.48, f32[32,48,1024]{2,0,1:T(8,128)S(1)} %bitcast.312), kind=kOutput, calls=%fused_computation.151 | convolution fusion | flops 472690400 | bytes 12845056 | tf_op jit(solution)/shard_map/kmc,mj->kjc/dot_general | solution.py:51
  370.7 8.4 %fusion.130 = f32[25,32,1024]{2,0,1:T(8,128)} fusion(f32[25,32,1024]{2,0,1:T(8,128)S(1)} %fusion.24, f32[32,48,1024]{2,0,1:T(8,128)S(1)} %bitcast.308), kind=kOutput, calls=%fused_computation.155 | convolution fusion | flops 472690400 | bytes 12845056 | tf_op jit(solution)/shard_map/kmc,mj->kjc/dot_general | solution.py:51
  379.1 19.3 %fusion.81 = (f32[1,32,25,1024]{3,2,1,0:T(8,128)}, f32[1,32,25,1024]{3,2,1,0:T(8,128)}, f32[1,32,25,1024]{3,2,1,0:T(8,128)}, f32[1,32,25,1024]{3,2,1,0:T(8,128)}) fusion(f32[25,32,1024]{2,0,1:T(8,128)S(1)} %fusion.136, f32[25,32,1024]{2,0,1:T(8,128)} %copy-done.3, f32[25,32,1024]{2,0,1:T(8,128)} %fusion.118, f32[25,32,1024]{2,0,1:T(8,128)} %copy-done.4, ...), kind=kOutput, calls=%fused_computation.116 | convolution fusion | flops 483338816 | bytes 39059456 | tf_op jit(solution)/shard_map/kmc,mj->kjc/dot_general | solution.py:48
  412.5 24.6 %fusion.67 = (f32[1,32,25,1024]{3,2,1,0:T(8,128)}, f32[1,32,25,1024]{3,2,1,0:T(8,128)}, f32[1,32,25,1024]{3,2,1,0:T(8,128)}, f32[1,32,25,1024]{3,2,1,0:T(8,128)}) fusion(f32[1,32,25,1024]{3,1,2,0:T(8,128)} %get-tuple-element.25, f32[1,32,25,1024]{3,1,2,0:T(8,128)} %get-tuple-element.24, f32[25,32,1024]{2,0,1:T(8,128)} %fusion.130, ...), kind=kOutput, calls=%fused_computation.97 | convolution fusion | flops 483338816 | bytes 39059456 | tf_op jit(solution)/shard_map/kmc,mj->kjc/dot_general | solution.py:48
  468.0 34.5 %fusion.1 = f32[48,1024,32]{1,2,0:T(8,128)} fusion(f32[32,48]{0,1:T(8,128)S(1)} %fusion.151, f32[32,48]{0,1:T(8,128)S(1)} %get-tuple-element.34, f32[48,32,1024]{2,0,1:T(8,128)S(1)} %fusion.102, f32[48,32,1024]{2,0,1:T(8,128)S(1)} %fusion.98, f32[48,32,1024]{2,0,1:T(8,128)S(1)} %fusion.100, f32[48,32,1024]{2,0,1:T(8,128)} %fusion.96), kind=kOutput, calls=%fused_computation.9 | convolution fusion | flops 611858432 | bytes 31469568 | tf_op jit(solution)/shard_map/nk,kmc->cnm/dot_general | solution.py:83
  502.5 37.9 %multiply_bitcast_fusion = f32[1024,32,48]{0,1,2:T(8,128)} fusion(f32[48,1024,32]{1,2,0:T(8,128)} %fusion.1, f32[32,48]{0,1:T(8,128)S(1)} %fusion.151, f32[32,48]{0,1:T(8,128)S(1)} %get-tuple-element.34, f32[48,32,1024]{2,0,1:T(8,128)S(1)} %fusion.102, f32[48,32,1024]{2,0,1:T(8,128)S(1)} %fusion.98, f32[48,32,1024]{2,0,1:T(8,128)} %copy-done.2, ...), kind=kOutput, calls=%fused_computation.26 | convolution fusion | flops 615004160 | bytes 37761024 | tf_op jit(solution)/shard_map/nk,kmc->cnm/dot_general | solution.py:83
  549.4 42.9 %all-to-all-start = ((f32[16,64,768]{2,1,0:T(8,128)}), f32[16,64,768]{2,1,0:T(8,128)}, u32[]{:S(2)}, u32[]{:S(2)}) async-start(f32[16,64,768]{2,1,0:T(8,128)} %bitcast.46), calls=%async_computation | async-start | bytes 6291456 | tf_op jit(solution)/shard_map/all_to_all | solution.py:145
  623.8 29.8 %fusion.10 = f32[32,48,1024]{2,0,1:T(8,128)} fusion(f32[32,48]{0,1:T(8,128)S(1)} %fusion.151, f32[32,48]{0,1:T(8,128)S(1)} %get-tuple-element.34, f32[48,32,1024]{2,0,1:T(8,128)S(1)} %fusion.94, f32[48,32,1024]{2,0,1:T(8,128)S(1)} %fusion.90, f32[48,32,1024]{2,0,1:T(8,128)S(1)} %fusion.92, f32[48,32,1024]{2,0,1:T(8,128)} %fusion.88), kind=kOutput, calls=%fused_computation.19 | convolution fusion | flops 611858432 | bytes 31469568 | tf_op jit(solution)/shard_map/nk,kmc->nmc/dot_general | solution.py:87
  653.6 30.0 %fusion.7 = f32[32,48,1024]{2,0,1:T(8,128)} fusion(f32[32,48]{0,1:T(8,128)S(1)} %fusion.151, f32[32,48]{0,1:T(8,128)S(1)} %get-tuple-element.34, f32[48,32,1024]{2,0,1:T(8,128)S(1)} %fusion.94, f32[48,32,1024]{2,0,1:T(8,128)S(1)} %fusion.90, f32[48,32,1024]{2,0,1:T(8,128)S(1)} %fusion.92, f32[48,32,1024]{2,0,1:T(8,128)} %fusion.88), kind=kOutput, calls=%fused_computation.17 | convolution fusion | flops 611858432 | bytes 31469568 | tf_op jit(solution)/shard_map/nk,kmc->nmc/dot_general | solution.py:87
  (102 shorter events, 135.5 us)
Async XLA Ops:
  7.2 96.2 %all-gather.2.cloned.1.call-start = ((), (), s32[]{:S(2)}) async-start(), calls=%async_computation.1 | async-start | bytes 6684672 | tf_op jit(solution)/shard_map/all_gather | solution.py:109
  7.9 7.8 %collective-permute-start.2 = (f32[768,1024]{1,0:T(8,128)}, f32[768,1024]{1,0:T(8,128)S(1)}, u32[]{:S(2)}, u32[]{:S(2)}) collective-permute-start(f32[768,1024]{1,0:T(8,128)} %param.6), channel_id=1, source_target_pairs={{2,0},{4,2},{6,4},{8,6},{10,8},{12,10},{14,12},{16,14},{18,16},{20... | collective-permute-start | bytes 9437192 | tf_op jit(solution)/shard_map/ppermute | solution.py:13
  9.2 9.3 %collective-permute-start = (f32[768,1024]{1,0:T(8,128)}, f32[768,1024]{1,0:T(8,128)S(1)}, u32[]{:S(2)}, u32[]{:S(2)}) collective-permute-start(f32[768,1024]{1,0:T(8,128)} %param.5), channel_id=1, source_target_pairs={{0,2},{2,4},{4,6},{6,8},{8,10},{10,12},{12,14},{14,16},{16,18},{18... | collective-permute-start | bytes 9437192 | tf_op jit(solution)/shard_map/ppermute | solution.py:13
  13.3 5.3 copy-start.7
  18.5 21.3 %copy-start = (f32[1536,1024]{1,0:T(8,128)}, f32[1536,1024]{1,0:T(8,128)S(1)}, u32[]{:S(2)}) copy-start(f32[1536,1024]{1,0:T(8,128)S(1)} %pad_maximum_fusion.3) | copy-start | bytes 18874372
  39.8 63.6 %copy-start.8 = (f32[1024]{0:T(1024)S(1)}, f32[1024]{0:T(1024)}, u32[]{:S(2)}) copy-start(f32[1024]{0:T(1024)} %param.8) | copy-start | bytes 12292
  39.8 63.6 %copy-start.9 = (pred[1536]{0:T(1024)(128)(4,1)S(1)}, pred[1536]{0:T(1024)(128)(4,1)}, u32[]{:S(2)}) copy-start(pred[1536]{0:T(1024)(128)(4,1)} %constant.109.clone.1) | copy-start | bytes 4612
  190.0 10.7 %copy-start.1 = (f32[32,48,1024]{2,0,1:T(8,128)S(1)}, f32[32,48,1024]{2,0,1:T(8,128)}, u32[]{:S(2)}) copy-start(f32[32,48,1024]{2,0,1:T(8,128)} %get-tuple-element.13) | copy-start | bytes 18874372
  190.0 19.0 %slice-start.8 = ((s8[6291456]{0:T(1024)(128)(4,1)}), s8[4194304]{0:T(1024)(128)(4,1)S(1)}, s32[]{:S(2)}) async-start(s8[6291456]{0:T(1024)(128)(4,1)} %bitcast.305), calls=%async_computation.10 | async-start | bytes 8388608
  200.8 8.3 %slice-start.9 = ((s8[6291456]{0:T(1024)(128)(4,1)}), s8[2097152]{0:T(1024)(128)(4,1)S(1)}, s32[]{:S(2)}) async-start(s8[6291456]{0:T(1024)(128)(4,1)} %bitcast.305), calls=%async_computation.11 | async-start | bytes 4194304
  209.0 16.7 %slice-start.2 = ((s8[6291456]{0:T(1024)(128)(4,1)}), s8[4194304]{0:T(1024)(128)(4,1)S(1)}, s32[]{:S(2)}) async-start(s8[6291456]{0:T(1024)(128)(4,1)} %bitcast.297), calls=%async_computation.4 | async-start | bytes 8388608
  217.6 8.1 %slice-start.3 = ((s8[6291456]{0:T(1024)(128)(4,1)}), s8[2097152]{0:T(1024)(128)(4,1)S(1)}, s32[]{:S(2)}) async-start(s8[6291456]{0:T(1024)(128)(4,1)} %bitcast.297), calls=%async_computation.5 | async-start | bytes 4194304
  225.7 8.4 %copy-start.6 = (f32[25,32,1024]{2,0,1:T(8,128)S(1)}, f32[25,32,1024]{2,0,1:T(8,128)}, u32[]{:S(2)}) copy-start(f32[25,32,1024]{2,0,1:T(8,128)} %fusion.14) | copy-start | bytes 9830404
  234.2 24.4 %slice-start = ((s8[6291456]{0:T(1024)(128)(4,1)}), s8[4194304]{0:T(1024)(128)(4,1)S(1)}, s32[]{:S(2)}) async-start(s8[6291456]{0:T(1024)(128)(4,1)} %bitcast.295), calls=%async_computation.2 | async-start | bytes 8388608
  242.3 4.7 copy-start.3
  242.3 16.2 %slice-start.1 = ((s8[6291456]{0:T(1024)(128)(4,1)}), s8[2097152]{0:T(1024)(128)(4,1)S(1)}, s32[]{:S(2)}) async-start(s8[6291456]{0:T(1024)(128)(4,1)} %bitcast.295), calls=%async_computation.3 | async-start | bytes 4194304
  247.0 11.6 %copy-start.5 = (f32[25,32,1024]{2,0,1:T(8,128)S(1)}, f32[25,32,1024]{2,0,1:T(8,128)}, u32[]{:S(2)}) copy-start(f32[25,32,1024]{2,0,1:T(8,128)} %fusion.38) | copy-start | bytes 9830404
  257.3 141.2 %collective-permute-start.3 = (f32[2,32,25,1024]{3,1,2,0:T(8,128)}, f32[2,32,25,1024]{3,1,2,0:T(8,128)}, u32[]{:S(2)}, u32[]{:S(2)}) collective-permute-start(f32[2,32,25,1024]{3,1,2,0:T(8,128)} %copy.136), channel_id=1, source_target_pairs={{2,0},{4,2},{6,4},{8,6},{10,8},{12,10},{14,12},{16,14},{18,16},{20... | collective-permute-start | bytes 19660808 | tf_op jit(solution)/shard_map/ppermute | solution.py:13
  266.7 8.8 %copy-start.4 = (f32[25,32,1024]{2,0,1:T(8,128)}, f32[25,32,1024]{2,0,1:T(8,128)S(1)}, u32[]{:S(2)}) copy-start(f32[25,32,1024]{2,0,1:T(8,128)S(1)} %fusion.121) | copy-start | bytes 9830404
  266.7 62.5 %slice-start.6 = ((s8[6291456]{0:T(1024)(128)(4,1)}), s8[2097152]{0:T(1024)(128)(4,1)S(1)}, s32[]{:S(2)}) async-start(s8[6291456]{0:T(1024)(128)(4,1)} %bitcast.301), calls=%async_computation.8 | async-start | bytes 4194304
  275.5 53.7 %slice-start.7 = ((s8[6291456]{0:T(1024)(128)(4,1)}), s8[4194304]{0:T(1024)(128)(4,1)S(1)}, s32[]{:S(2)}) async-start(s8[6291456]{0:T(1024)(128)(4,1)} %bitcast.301), calls=%async_computation.9 | async-start | bytes 8388608
  292.5 113.0 %collective-permute-start.1 = (f32[2,32,25,1024]{3,1,2,0:T(8,128)}, f32[2,32,25,1024]{3,1,2,0:T(8,128)}, u32[]{:S(2)}, u32[]{:S(2)}) collective-permute-start(f32[2,32,25,1024]{3,1,2,0:T(8,128)} %copy.120), channel_id=1, source_target_pairs={{0,2},{2,4},{4,6},{6,8},{8,10},{10,12},{12,14},{14,16},{16,18},{18... | collective-permute-start | bytes 19660808 | tf_op jit(solution)/shard_map/ppermute | solution.py:13
  329.2 16.5 %slice-start.4 = ((s8[6291456]{0:T(1024)(128)(4,1)}), s8[4194304]{0:T(1024)(128)(4,1)S(1)}, s32[]{:S(2)}) async-start(s8[6291456]{0:T(1024)(128)(4,1)} %bitcast.299), calls=%async_computation.6 | async-start | bytes 8388608
  337.3 8.5 %slice-start.5 = ((s8[6291456]{0:T(1024)(128)(4,1)}), s8[2097152]{0:T(1024)(128)(4,1)S(1)}, s32[]{:S(2)}) async-start(s8[6291456]{0:T(1024)(128)(4,1)} %bitcast.299), calls=%async_computation.7 | async-start | bytes 4194304
  345.8 16.6 %slice-start.14 = ((s8[6291456]{0:T(1024)(128)(4,1)}), s8[4194304]{0:T(1024)(128)(4,1)S(1)}, s32[]{:S(2)}) async-start(s8[6291456]{0:T(1024)(128)(4,1)} %bitcast.311), calls=%async_computation.16 | async-start | bytes 8388608
  353.8 8.5 %slice-start.15 = ((s8[6291456]{0:T(1024)(128)(4,1)}), s8[2097152]{0:T(1024)(128)(4,1)S(1)}, s32[]{:S(2)}) async-start(s8[6291456]{0:T(1024)(128)(4,1)} %bitcast.311), calls=%async_computation.17 | async-start | bytes 4194304
  353.9 16.9 %slice-start.10 = ((s8[6291456]{0:T(1024)(128)(4,1)}), s8[2097152]{0:T(1024)(128)(4,1)S(1)}, s32[]{:S(2)}) async-start(s8[6291456]{0:T(1024)(128)(4,1)} %bitcast.307), calls=%async_computation.12 | async-start | bytes 4194304
  362.3 8.4 %slice-start.11 = ((s8[6291456]{0:T(1024)(128)(4,1)}), s8[4194304]{0:T(1024)(128)(4,1)S(1)}, s32[]{:S(2)}) async-start(s8[6291456]{0:T(1024)(128)(4,1)} %bitcast.307), calls=%async_computation.13 | async-start | bytes 8388608
  398.4 14.1 %slice-start.12 = ((s8[6291456]{0:T(1024)(128)(4,1)}), s8[4194304]{0:T(1024)(128)(4,1)S(1)}, s32[]{:S(2)}) async-start(s8[6291456]{0:T(1024)(128)(4,1)} %bitcast.309), calls=%async_computation.14 | async-start | bytes 8388608
  405.4 7.1 %slice-start.13 = ((s8[6291456]{0:T(1024)(128)(4,1)}), s8[2097152]{0:T(1024)(128)(4,1)S(1)}, s32[]{:S(2)}) async-start(s8[6291456]{0:T(1024)(128)(4,1)} %bitcast.309), calls=%async_computation.15 | async-start | bytes 4194304
  460.7 7.3 %copy-start.2 = (f32[48,32,1024]{2,0,1:T(8,128)}, f32[48,32,1024]{2,0,1:T(8,128)S(1)}, u32[]{:S(2)}) copy-start(f32[48,32,1024]{2,0,1:T(8,128)S(1)} %fusion.100) | copy-start | bytes 18874372
  549.4 141.5 %all-to-all-start = ((f32[16,64,768]{2,1,0:T(8,128)}), f32[16,64,768]{2,1,0:T(8,128)}, u32[]{:S(2)}, u32[]{:S(2)}) async-start(f32[16,64,768]{2,1,0:T(8,128)} %bitcast.46), calls=%async_computation | async-start | bytes 6291456 | tf_op jit(solution)/shard_map/all_to_all | solution.py:145
Sparse Core Ops, SparseCore 0:
  10.3 93.1 all-gather.1
where the time goes:
time: 710 us; the launch traced here: 702 us
  matrix products  455 us (64%)
  starting transfers between devices  85.3 us (12%)
  waiting for transfers between devices  56.4 us (8%)
  local copies, waits for them, and re-layouts  52.3 us (7%)
  other arithmetic  38.3 us (5%)
  between operations  15 us (2%)
    dot_general x4, matrix products, forward_real(): jnp.einsum('kn,nmc->kmc', sin_first, grid_view, precision=PRECISE)  70.7 us
    dot_general x4, matrix products, forward_real(): jnp.einsum('kmc,mj->kjc', rot_real, cos_second, precision=PRECISE)  60.1 us
    all_gather x1, waiting for transfers between devices, local(): piece_rows = lax.all_gather(filter_rows, 'ctx', axis=0, tiled=True)  53.3 us
    all_to_all x1, starting transfers between devices, local(): lax.all_to_all(local_grad, 'ctx', split_axis=0, concat_axis=1, tiled=True)  42.9 us
    ppermute x4, starting transfers between devices, passed_along(): lax.ppermute(value, axis, [(source, source + steps) for source in range(i...  42.4 us
    dot_general x4, matrix products, forward_real(): jnp.einsum('kn,nmc->kmc', cos_first, grid_view, precision=PRECISE)  41.1 us
    dot_general x1, matrix products, inverse_real(): jnp.einsum('nk,kmc->cnm', sin_first, rot_imag, precision=PRECISE)  37.9 us
    dot_general x4, matrix products, forward_real(): jnp.einsum('kmc,mj->kjc', rot_imag, cos_second, precision=PRECISE)  34.9 us
  transfers between devices with their start and end apart: 6, of which 2 were waited for; matrix products, arithmetic and copies ran while one was open for 35% of the time, Pallas kernels for 0%

commit v1 on v0

--- a/solution.py
+++ b/solution.py
@@ -5,6 +5,9 @@
 from jax.sharding import PartitionSpec as P
 
 PRECISE = lax.Precision.HIGHEST
+run_tokens = lambda vec: jnp.concatenate(
+    lax.all_to_all(jnp.stack(jnp.split(vec, lax.axis_size("ctx"), 0), 0), "ctx", 0, 0), 1
+)
 
 
 def passed_along(value, axis, steps):
@@ -142,7 +145,7 @@
     outputs = lax.slice_in_dim(forward_time, block_len, 2 * block_len, axis=0)
     backward_time = inverse_real(totals[1], factors, True)
     local_grad = lax.slice_in_dim(backward_time, 0, block_len, axis=1)
-    input_grad = lax.all_to_all(local_grad, "ctx", split_axis=0, concat_axis=1, tiled=True)
+    input_grad = run_tokens(local_grad)
     return (outputs, input_grad)
 
 

time: 710 us -> 727 us (1.024)
  local copies, waits for them, and re-layouts: 52.3 us -> 69.7 us
    unnamed x52 -> x67, local copies, waits for them, and re-layouts: 0.47 us -> 13.4 us
  transfers between devices with their start and end apart: 6 -> 6, of which waited for: 2 -> 2; matrix products, arithmetic and copies ran while one was open for 35% -> 34% of each run, Pallas kernels for 0% -> 0%
where the time goes in v1:
time: 727 us; the launch traced here: 719 us
  matrix products  455 us (63%)
  starting transfers between devices  85.3 us (12%)
  local copies, waits for them, and re-layouts  69.7 us (10%)
  waiting for transfers between devices  56.4 us (8%)
  other arithmetic  38.3 us (5%)
  between operations  15 us (2%)
    dot_general x4, matrix products, forward_real(): jnp.einsum('kn,nmc->kmc', sin_first, grid_view, precision=PRECISE)  70.7 us
    dot_general x4, matrix products, forward_real(): jnp.einsum('kmc,mj->kjc', rot_real, cos_second, precision=PRECISE)  60.1 us
    all_gather x1, waiting for transfers between devices, local(): piece_rows = lax.all_gather(filter_rows, 'ctx', axis=0, tiled=True)  53.3 us
    all_to_all x1, starting transfers between devices, lax.all_to_all(jnp.stack(jnp.split(vec, lax.axis_size('ctx'), 0), 0), 'ct...  42.9 us
    ppermute x4, starting transfers between devices, passed_along(): lax.ppermute(value, axis, [(source, source + steps) for source in range(i...  42.4 us
    dot_general x4, matrix products, forward_real(): jnp.einsum('kn,nmc->kmc', cos_first, grid_view, precision=PRECISE)  41.1 us
    dot_general x1, matrix products, inverse_real(): jnp.einsum('nk,kmc->cnm', sin_first, rot_imag, precision=PRECISE)  37.9 us
    dot_general x4, matrix products, forward_real(): jnp.einsum('kmc,mj->kjc', rot_imag, cos_second, precision=PRECISE)  34.9 us
  transfers between devices with their start and end apart: 6, of which 2 were waited for; matrix products, arithmetic and copies ran while one was open for 34% of the time, Pallas kernels for 0%

profile of v1, /device:TPU:0, one launch (start us, length us, event | category | flops | bytes accessed | tf_op | source)
XLA Modules:
  0.0 719.5 jit_solution(186891245333383068)
XLA Ops:
  19.7 10.0 %fusion.44 = f32[32,48,1024]{2,0,1:T(8,128)} fusion(f32[32,48,1024]{2,1,0:T(8,128)S(1)} %bitcast.380), kind=kOutput, calls=%fused_computation.69 | convolution fusion | flops 603995136 | bytes 12582912 | tf_op jit(solution)/shard_map/kn,nmc->kmc/dot_general | solution.py:46
  29.7 10.1 %fusion.46 = f32[32,48,1024]{2,0,1:T(8,128)} fusion(f32[32,48,1024]{2,1,0:T(8,128)S(1)} %bitcast.381), kind=kOutput, calls=%fused_computation.71 | convolution fusion | flops 603994112 | bytes 12582912 | tf_op jit(solution)/shard_map/kn,nmc->kmc/dot_general | solution.py:45
  39.8 10.3 %fusion.22 = f32[32,48,1024]{2,0,1:T(8,128)} fusion(f32[32,48,1024]{2,1,0:T(8,128)S(1)} %bitcast.366), kind=kOutput, calls=%fused_computation.47 | convolution fusion | flops 603994112 | bytes 12582912 | tf_op jit(solution)/shard_map/kn,nmc->kmc/dot_general | solution.py:45
  50.1 53.3 %all-gather.2.cloned.1.call-done = f32[1536,1024]{1,0:T(8,128)} async-done(((f32[96,1024]{1,0:T(8,128)}), f32[1536,1024]{1,0:T(8,128)}) %all-gather.2.cloned.1.call-update) | async-done | bytes 6291472 | tf_op jit(solution)/shard_map/all_gather | solution.py:112
  108.7 10.1 %fusion.32 = f32[32,48,1024]{2,0,1:T(8,128)} fusion(f32[32,48,1024]{2,1,0:T(8,128)S(1)} %bitcast.378), kind=kOutput, calls=%fused_computation.57 | convolution fusion | flops 603995136 | bytes 12582912 | tf_op jit(solution)/shard_map/kn,nmc->kmc/dot_general | solution.py:46
  118.7 10.4 %fusion.34 = f32[32,48,1024]{2,0,1:T(8,128)} fusion(f32[32,48,1024]{2,1,0:T(8,128)S(1)} %bitcast.379), kind=kOutput, calls=%fused_computation.59 | convolution fusion | flops 603994112 | bytes 12582912 | tf_op jit(solution)/shard_map/kn,nmc->kmc/dot_general | solution.py:45
  129.2 10.1 %fusion.56 = f32[32,48,1024]{2,0,1:T(8,128)} fusion(f32[32,48,1024]{2,1,0:T(8,128)S(1)} %bitcast.376), kind=kOutput, calls=%fused_computation.81 | convolution fusion | flops 603995136 | bytes 12582912 | tf_op jit(solution)/shard_map/kn,nmc->kmc/dot_general | solution.py:46
  139.2 10.3 %fusion.58 = f32[32,48,1024]{2,0,1:T(8,128)} fusion(f32[32,48,1024]{2,1,0:T(8,128)S(1)} %bitcast.377), kind=kOutput, calls=%fused_computation.83 | convolution fusion | flops 603994112 | bytes 12582912 | tf_op jit(solution)/shard_map/kn,nmc->kmc/dot_general | solution.py:45
  149.5 40.5 %multiply_subtract_fusion = (f32[32,48,1024]{2,0,1:T(8,128)}, f32[32,48,1024]{2,0,1:T(8,128)}, f32[32,48,1024]{2,0,1:T(8,128)}, f32[32,48,1024]{2,0,1:T(8,128)},...) fusion(f32[32,48,1024]{2,0,1:T(8,128)} %fusion.22, ...), kind=kOutput, calls=%fused_computation.28 | convolution fusion | flops 641743872 | bytes 100675584 | tf_op jit(solution)/shard_map/kn,nmc->kmc/dot_general | solution.py:46
  190.1 10.7 %fusion.12 = f32[25,32,1024]{2,0,1:T(8,128)S(1)} fusion(f32[32,48,1024]{2,0,1:T(8,128)} %get-tuple-element.15), kind=kOutput, calls=%fused_computation.37 | convolution fusion | flops 471870016 | bytes 9568256 | tf_op jit(solution)/shard_map/kmc,mj->kjc/dot_general | solution.py:54
  200.8 8.2 %fusion.14 = f32[25,32,1024]{2,0,1:T(8,128)} fusion(f32[32,48,1024]{2,0,1:T(8,128)S(1)} %copy-done.1), kind=kOutput, calls=%fused_computation.39 | convolution fusion | flops 471871200 | bytes 9568256 | tf_op jit(solution)/shard_map/kmc,mj->kjc/dot_general | solution.py:51
  209.0 8.6 %fusion.38 = f32[25,32,1024]{2,0,1:T(8,128)} fusion(f32[32,48,1024]{2,0,1:T(8,128)S(1)} %bitcast.369), kind=kOutput, calls=%fused_computation.63 | convolution fusion | flops 471871200 | bytes 9568256 | tf_op jit(solution)/shard_map/kmc,mj->kjc/dot_general | solution.py:51
  217.6 8.1 %fusion.36 = f32[25,32,1024]{2,0,1:T(8,128)S(1)} fusion(f32[32,48,1024]{2,0,1:T(8,128)S(1)} %bitcast.369), kind=kOutput, calls=%fused_computation.61 | convolution fusion | flops 471870016 | bytes 9568256 | tf_op jit(solution)/shard_map/kmc,mj->kjc/dot_general | solution.py:54
  225.7 8.4 %fusion.136 = f32[25,32,1024]{2,0,1:T(8,128)S(1)} fusion(f32[25,32,1024]{2,0,1:T(8,128)S(1)} %fusion.12, f32[32,48,1024]{2,0,1:T(8,128)S(1)} %bitcast.361), kind=kOutput, calls=%fused_computation.157 | convolution fusion | flops 472690400 | bytes 12845056 | tf_op jit(solution)/shard_map/kmc,mj->kjc/dot_general | solution.py:54
  234.2 8.1 %fusion.133 = f32[25,32,1024]{2,0,1:T(8,128)S(1)} fusion(f32[25,32,1024]{2,0,1:T(8,128)S(1)} %copy-done.6, f32[32,48,1024]{2,0,1:T(8,128)S(1)} %bitcast.361), kind=kOutput, calls=%fused_computation.156 | convolution fusion | flops 472689216 | bytes 12845056 | tf_op jit(solution)/shard_map/kmc,mj->kjc/dot_general | solution.py:51
  247.0 10.3 %copy.156 = f32[2,32,25,1024]{3,1,2,0:T(8,128)} copy(f32[2,32,25,1024]{3,2,1,0:T(8,128)} %pad_maximum_fusion.1) | data formatting | bytes 13107200 | tf_op jit(solution)/shard_map/stack | solution.py:57
  258.6 8.1 %fusion.121 = f32[25,32,1024]{2,0,1:T(8,128)S(1)} fusion(f32[25,32,1024]{2,0,1:T(8,128)S(1)} %copy-done.5, f32[32,48,1024]{2,0,1:T(8,128)S(1)} %bitcast.359), kind=kOutput, calls=%fused_computation.152 | convolution fusion | flops 472689216 | bytes 12845056 | tf_op jit(solution)/shard_map/kmc,mj->kjc/dot_general | solution.py:51
  266.7 8.8 %fusion.124 = f32[25,32,1024]{2,0,1:T(8,128)} fusion(f32[25,32,1024]{2,0,1:T(8,128)S(1)} %fusion.36, f32[32,48,1024]{2,0,1:T(8,128)S(1)} %bitcast.359), kind=kOutput, calls=%fused_computation.153 | convolution fusion | flops 472690400 | bytes 12845056 | tf_op jit(solution)/shard_map/kmc,mj->kjc/dot_general | solution.py:54
  282.6 9.9 %copy.140 = f32[2,32,25,1024]{3,1,2,0:T(8,128)} copy(f32[2,32,25,1024]{3,2,1,0:T(8,128)} %pad_maximum_fusion) | data formatting | bytes 13107200 | tf_op jit(solution)/shard_map/stack | solution.py:57
  292.5 36.6 %collective-permute-start.1 = (f32[2,32,25,1024]{3,1,2,0:T(8,128)}, f32[2,32,25,1024]{3,1,2,0:T(8,128)}, u32[]{:S(2)}, u32[]{:S(2)}) collective-permute-start(f32[2,32,25,1024]{3,1,2,0:T(8,128)} %copy.140), channel_id=1, source_target_pairs={{0,2},{2,4},{4,6},{6,8},{8,10},{10,12},{12,14},{14,16},{16,18},{18... | collective-permute-start | bytes 19660808 | tf_op jit(solution)/shard_map/ppermute | solution.py:16
  329.2 8.1 %fusion.48 = f32[25,32,1024]{2,0,1:T(8,128)S(1)} fusion(f32[32,48,1024]{2,0,1:T(8,128)S(1)} %bitcast.365), kind=kOutput, calls=%fused_computation.73 | convolution fusion | flops 471870016 | bytes 9568256 | tf_op jit(solution)/shard_map/kmc,mj->kjc/dot_general | solution.py:54
  337.3 8.4 %fusion.50 = f32[25,32,1024]{2,0,1:T(8,128)} fusion(f32[32,48,1024]{2,0,1:T(8,128)S(1)} %bitcast.365), kind=kOutput, calls=%fused_computation.75 | convolution fusion | flops 471871200 | bytes 9568256 | tf_op jit(solution)/shard_map/kmc,mj->kjc/dot_general | solution.py:51
  353.9 8.5 %fusion.26 = f32[25,32,1024]{2,0,1:T(8,128)} fusion(f32[32,48,1024]{2,0,1:T(8,128)S(1)} %bitcast.363), kind=kOutput, calls=%fused_computation.51 | convolution fusion | flops 471871200 | bytes 9568256 | tf_op jit(solution)/shard_map/kmc,mj->kjc/dot_general | solution.py:51
  362.3 8.4 %fusion.118 = f32[25,32,1024]{2,0,1:T(8,128)} fusion(f32[25,32,1024]{2,0,1:T(8,128)S(1)} %fusion.48, f32[32,48,1024]{2,0,1:T(8,128)S(1)} %bitcast.375), kind=kOutput, calls=%fused_computation.151 | convolution fusion | flops 472690400 | bytes 12845056 | tf_op jit(solution)/shard_map/kmc,mj->kjc/dot_general | solution.py:54
  370.7 8.4 %fusion.130 = f32[25,32,1024]{2,0,1:T(8,128)} fusion(f32[25,32,1024]{2,0,1:T(8,128)S(1)} %fusion.24, f32[32,48,1024]{2,0,1:T(8,128)S(1)} %bitcast.371), kind=kOutput, calls=%fused_computation.155 | convolution fusion | flops 472690400 | bytes 12845056 | tf_op jit(solution)/shard_map/kmc,mj->kjc/dot_general | solution.py:54
  379.1 19.3 %fusion.81 = (f32[1,32,25,1024]{3,2,1,0:T(8,128)}, f32[1,32,25,1024]{3,2,1,0:T(8,128)}, f32[1,32,25,1024]{3,2,1,0:T(8,128)}, f32[1,32,25,1024]{3,2,1,0:T(8,128)}) fusion(f32[25,32,1024]{2,0,1:T(8,128)S(1)} %fusion.136, f32[25,32,1024]{2,0,1:T(8,128)} %copy-done.3, f32[25,32,1024]{2,0,1:T(8,128)} %fusion.118, f32[25,32,1024]{2,0,1:T(8,128)} %copy-done.4, ...), kind=kOutput, calls=%fused_computation.116 | convolution fusion | flops 483338816 | bytes 39059456 | tf_op jit(solution)/shard_map/kmc,mj->kjc/dot_general | solution.py:51
  412.5 24.6 %fusion.67 = (f32[1,32,25,1024]{3,2,1,0:T(8,128)}, f32[1,32,25,1024]{3,2,1,0:T(8,128)}, f32[1,32,25,1024]{3,2,1,0:T(8,128)}, f32[1,32,25,1024]{3,2,1,0:T(8,128)}) fusion(f32[1,32,25,1024]{3,1,2,0:T(8,128)} %get-tuple-element.27, f32[1,32,25,1024]{3,1,2,0:T(8,128)} %get-tuple-element.26, f32[25,32,1024]{2,0,1:T(8,128)} %fusion.130, ...), kind=kOutput, calls=%fused_computation.97 | convolution fusion | flops 483338816 | bytes 39059456 | tf_op jit(solution)/shard_map/kmc,mj->kjc/dot_general | solution.py:51
  468.0 34.5 %fusion.1 = f32[48,1024,32]{1,2,0:T(8,128)} fusion(f32[32,48]{0,1:T(8,128)S(1)} %fusion.167, f32[32,48]{0,1:T(8,128)S(1)} %get-tuple-element.36, f32[48,32,1024]{2,0,1:T(8,128)S(1)} %fusion.102, f32[48,32,1024]{2,0,1:T(8,128)S(1)} %fusion.98, f32[48,32,1024]{2,0,1:T(8,128)S(1)} %fusion.100, f32[48,32,1024]{2,0,1:T(8,128)} %fusion.96), kind=kOutput, calls=%fused_computation.9 | convolution fusion | flops 611858432 | bytes 31469568 | tf_op jit(solution)/shard_map/nk,kmc->cnm/dot_general | solution.py:86
  502.5 37.9 %multiply_bitcast_fusion = f32[1024,32,48]{0,1,2:T(8,128)} fusion(f32[48,1024,32]{1,2,0:T(8,128)} %fusion.1, f32[32,48]{0,1:T(8,128)S(1)} %fusion.167, f32[32,48]{0,1:T(8,128)S(1)} %get-tuple-element.36, f32[48,32,1024]{2,0,1:T(8,128)S(1)} %fusion.102, f32[48,32,1024]{2,0,1:T(8,128)S(1)} %fusion.98, f32[48,32,1024]{2,0,1:T(8,128)} %copy-done.2, ...), kind=kOutput, calls=%fused_computation.26 | convolution fusion | flops 615004160 | bytes 37761024 | tf_op jit(solution)/shard_map/nk,kmc->cnm/dot_general | solution.py:86
  566.8 42.9 %all-to-all-start = ((f32[16,64,768]{2,1,0:T(8,128)}), f32[16,64,768]{2,1,0:T(8,128)}, u32[]{:S(2)}, u32[]{:S(2)}) async-start(f32[16,64,768]{2,1,0:T(8,128)} %copy.164), calls=%async_computation | async-start | bytes 6291456 | tf_op jit(solution)/shard_map/all_to_all | solution.py:9
  641.1 29.8 %fusion.10 = f32[32,48,1024]{2,0,1:T(8,128)} fusion(f32[32,48]{0,1:T(8,128)S(1)} %fusion.167, f32[32,48]{0,1:T(8,128)S(1)} %get-tuple-element.36, f32[48,32,1024]{2,0,1:T(8,128)S(1)} %fusion.94, f32[48,32,1024]{2,0,1:T(8,128)S(1)} %fusion.90, f32[48,32,1024]{2,0,1:T(8,128)S(1)} %fusion.92, f32[48,32,1024]{2,0,1:T(8,128)} %fusion.88), kind=kOutput, calls=%fused_computation.19 | convolution fusion | flops 611858432 | bytes 31469568 | tf_op jit(solution)/shard_map/nk,kmc->nmc/dot_general | solution.py:90
  671.0 30.0 %fusion.7 = f32[32,48,1024]{2,0,1:T(8,128)} fusion(f32[32,48]{0,1:T(8,128)S(1)} %fusion.167, f32[32,48]{0,1:T(8,128)S(1)} %get-tuple-element.36, f32[48,32,1024]{2,0,1:T(8,128)S(1)} %fusion.94, f32[48,32,1024]{2,0,1:T(8,128)S(1)} %fusion.90, f32[48,32,1024]{2,0,1:T(8,128)S(1)} %fusion.92, f32[48,32,1024]{2,0,1:T(8,128)} %fusion.88), kind=kOutput, calls=%fused_computation.17 | convolution fusion | flops 611858432 | bytes 31469568 | tf_op jit(solution)/shard_map/nk,kmc->nmc/dot_general | solution.py:90
  (117 shorter events, 152.9 us)
Async XLA Ops:
  7.2 96.2 %all-gather.2.cloned.1.call-start = ((), (), s32[]{:S(2)}) async-start(), calls=%async_computation.1 | async-start | bytes 6684672 | tf_op jit(solution)/shard_map/all_gather | solution.py:112
  7.9 7.8 %collective-permute-start.2 = (f32[768,1024]{1,0:T(8,128)}, f32[768,1024]{1,0:T(8,128)S(1)}, u32[]{:S(2)}, u32[]{:S(2)}) collective-permute-start(f32[768,1024]{1,0:T(8,128)} %param.6), channel_id=1, source_target_pairs={{2,0},{4,2},{6,4},{8,6},{10,8},{12,10},{14,12},{16,14},{18,16},{20... | collective-permute-start | bytes 9437192 | tf_op jit(solution)/shard_map/ppermute | solution.py:16
  9.2 9.3 %collective-permute-start = (f32[768,1024]{1,0:T(8,128)}, f32[768,1024]{1,0:T(8,128)S(1)}, u32[]{:S(2)}, u32[]{:S(2)}) collective-permute-start(f32[768,1024]{1,0:T(8,128)} %param.5), channel_id=1, source_target_pairs={{0,2},{2,4},{4,6},{6,8},{8,10},{10,12},{12,14},{14,16},{16,18},{18... | collective-permute-start | bytes 9437192 | tf_op jit(solution)/shard_map/ppermute | solution.py:16
  13.3 5.3 copy-start.7
  18.5 21.3 %copy-start = (f32[1536,1024]{1,0:T(8,128)}, f32[1536,1024]{1,0:T(8,128)S(1)}, u32[]{:S(2)}) copy-start(f32[1536,1024]{1,0:T(8,128)S(1)} %pad_maximum_fusion.3) | copy-start | bytes 18874372
  39.8 63.6 %copy-start.8 = (f32[1024]{0:T(1024)S(1)}, f32[1024]{0:T(1024)}, u32[]{:S(2)}) copy-start(f32[1024]{0:T(1024)} %param.8) | copy-start | bytes 12292
  39.8 63.6 %copy-start.9 = (pred[1536]{0:T(1024)(128)(4,1)S(1)}, pred[1536]{0:T(1024)(128)(4,1)}, u32[]{:S(2)}) copy-start(pred[1536]{0:T(1024)(128)(4,1)} %constant.109.clone.1) | copy-start | bytes 4612
  190.0 10.7 %copy-start.1 = (f32[32,48,1024]{2,0,1:T(8,128)S(1)}, f32[32,48,1024]{2,0,1:T(8,128)}, u32[]{:S(2)}) copy-start(f32[32,48,1024]{2,0,1:T(8,128)} %get-tuple-element.15) | copy-start | bytes 18874372
  190.0 19.0 %slice-start.8 = ((s8[6291456]{0:T(1024)(128)(4,1)}), s8[4194304]{0:T(1024)(128)(4,1)S(1)}, s32[]{:S(2)}) async-start(s8[6291456]{0:T(1024)(128)(4,1)} %bitcast.368), calls=%async_computation.10 | async-start | bytes 8388608
  200.8 8.3 %slice-start.9 = ((s8[6291456]{0:T(1024)(128)(4,1)}), s8[2097152]{0:T(1024)(128)(4,1)S(1)}, s32[]{:S(2)}) async-start(s8[6291456]{0:T(1024)(128)(4,1)} %bitcast.368), calls=%async_computation.11 | async-start | bytes 4194304
  209.0 16.7 %slice-start.2 = ((s8[6291456]{0:T(1024)(128)(4,1)}), s8[4194304]{0:T(1024)(128)(4,1)S(1)}, s32[]{:S(2)}) async-start(s8[6291456]{0:T(1024)(128)(4,1)} %bitcast.360), calls=%async_computation.4 | async-start | bytes 8388608
  217.6 8.1 %slice-start.3 = ((s8[6291456]{0:T(1024)(128)(4,1)}), s8[2097152]{0:T(1024)(128)(4,1)S(1)}, s32[]{:S(2)}) async-start(s8[6291456]{0:T(1024)(128)(4,1)} %bitcast.360), calls=%async_computation.5 | async-start | bytes 4194304
  225.7 8.4 %copy-start.6 = (f32[25,32,1024]{2,0,1:T(8,128)S(1)}, f32[25,32,1024]{2,0,1:T(8,128)}, u32[]{:S(2)}) copy-start(f32[25,32,1024]{2,0,1:T(8,128)} %fusion.14) | copy-start | bytes 9830404
  234.2 24.4 %slice-start = ((s8[6291456]{0:T(1024)(128)(4,1)}), s8[4194304]{0:T(1024)(128)(4,1)S(1)}, s32[]{:S(2)}) async-start(s8[6291456]{0:T(1024)(128)(4,1)} %bitcast.358), calls=%async_computation.2 | async-start | bytes 8388608
  242.3 4.7 copy-start.3
  242.3 16.2 %slice-start.1 = ((s8[6291456]{0:T(1024)(128)(4,1)}), s8[2097152]{0:T(1024)(128)(4,1)S(1)}, s32[]{:S(2)}) async-start(s8[6291456]{0:T(1024)(128)(4,1)} %bitcast.358), calls=%async_computation.3 | async-start | bytes 4194304
  247.0 11.6 %copy-start.5 = (f32[25,32,1024]{2,0,1:T(8,128)S(1)}, f32[25,32,1024]{2,0,1:T(8,128)}, u32[]{:S(2)}) copy-start(f32[25,32,1024]{2,0,1:T(8,128)} %fusion.38) | copy-start | bytes 9830404
  257.3 141.2 %collective-permute-start.3 = (f32[2,32,25,1024]{3,1,2,0:T(8,128)}, f32[2,32,25,1024]{3,1,2,0:T(8,128)}, u32[]{:S(2)}, u32[]{:S(2)}) collective-permute-start(f32[2,32,25,1024]{3,1,2,0:T(8,128)} %copy.156), channel_id=1, source_target_pairs={{2,0},{4,2},{6,4},{8,6},{10,8},{12,10},{14,12},{16,14},{18,16},{20... | collective-permute-start | bytes 19660808 | tf_op jit(solution)/shard_map/ppermute | solution.py:16
  266.7 8.8 %copy-start.4 = (f32[25,32,1024]{2,0,1:T(8,128)}, f32[25,32,1024]{2,0,1:T(8,128)S(1)}, u32[]{:S(2)}) copy-start(f32[25,32,1024]{2,0,1:T(8,128)S(1)} %fusion.121) | copy-start | bytes 9830404
  266.7 62.5 %slice-start.6 = ((s8[6291456]{0:T(1024)(128)(4,1)}), s8[2097152]{0:T(1024)(128)(4,1)S(1)}, s32[]{:S(2)}) async-start(s8[6291456]{0:T(1024)(128)(4,1)} %bitcast.364), calls=%async_computation.8 | async-start | bytes 4194304
  275.5 53.7 %slice-start.7 = ((s8[6291456]{0:T(1024)(128)(4,1)}), s8[4194304]{0:T(1024)(128)(4,1)S(1)}, s32[]{:S(2)}) async-start(s8[6291456]{0:T(1024)(128)(4,1)} %bitcast.364), calls=%async_computation.9 | async-start | bytes 8388608
  292.5 113.0 %collective-permute-start.1 = (f32[2,32,25,1024]{3,1,2,0:T(8,128)}, f32[2,32,25,1024]{3,1,2,0:T(8,128)}, u32[]{:S(2)}, u32[]{:S(2)}) collective-permute-start(f32[2,32,25,1024]{3,1,2,0:T(8,128)} %copy.140), channel_id=1, source_target_pairs={{0,2},{2,4},{4,6},{6,8},{8,10},{10,12},{12,14},{14,16},{16,18},{18... | collective-permute-start | bytes 19660808 | tf_op jit(solution)/shard_map/ppermute | solution.py:16
  329.2 16.5 %slice-start.4 = ((s8[6291456]{0:T(1024)(128)(4,1)}), s8[4194304]{0:T(1024)(128)(4,1)S(1)}, s32[]{:S(2)}) async-start(s8[6291456]{0:T(1024)(128)(4,1)} %bitcast.362), calls=%async_computation.6 | async-start | bytes 8388608
  337.3 8.5 %slice-start.5 = ((s8[6291456]{0:T(1024)(128)(4,1)}), s8[2097152]{0:T(1024)(128)(4,1)S(1)}, s32[]{:S(2)}) async-start(s8[6291456]{0:T(1024)(128)(4,1)} %bitcast.362), calls=%async_computation.7 | async-start | bytes 4194304
  345.8 16.6 %slice-start.14 = ((s8[6291456]{0:T(1024)(128)(4,1)}), s8[4194304]{0:T(1024)(128)(4,1)S(1)}, s32[]{:S(2)}) async-start(s8[6291456]{0:T(1024)(128)(4,1)} %bitcast.374), calls=%async_computation.16 | async-start | bytes 8388608
  353.8 8.5 %slice-start.15 = ((s8[6291456]{0:T(1024)(128)(4,1)}), s8[2097152]{0:T(1024)(128)(4,1)S(1)}, s32[]{:S(2)}) async-start(s8[6291456]{0:T(1024)(128)(4,1)} %bitcast.374), calls=%async_computation.17 | async-start | bytes 4194304
  353.8 16.9 %slice-start.10 = ((s8[6291456]{0:T(1024)(128)(4,1)}), s8[2097152]{0:T(1024)(128)(4,1)S(1)}, s32[]{:S(2)}) async-start(s8[6291456]{0:T(1024)(128)(4,1)} %bitcast.370), calls=%async_computation.12 | async-start | bytes 4194304
  362.3 8.4 %slice-start.11 = ((s8[6291456]{0:T(1024)(128)(4,1)}), s8[4194304]{0:T(1024)(128)(4,1)S(1)}, s32[]{:S(2)}) async-start(s8[6291456]{0:T(1024)(128)(4,1)} %bitcast.370), calls=%async_computation.13 | async-start | bytes 8388608
  398.4 14.1 %slice-start.12 = ((s8[6291456]{0:T(1024)(128)(4,1)}), s8[4194304]{0:T(1024)(128)(4,1)S(1)}, s32[]{:S(2)}) async-start(s8[6291456]{0:T(1024)(128)(4,1)} %bitcast.372), calls=%async_computation.14 | async-start | bytes 8388608
  405.4 7.1 slice-start.13
  460.7 7.3 %copy-start.2 = (f32[48,32,1024]{2,0,1:T(8,128)}, f32[48,32,1024]{2,0,1:T(8,128)S(1)}, u32[]{:S(2)}) copy-start(f32[48,32,1024]{2,0,1:T(8,128)S(1)} %fusion.100) | copy-start | bytes 18874372
  566.8 141.6 %all-to-all-start = ((f32[16,64,768]{2,1,0:T(8,128)}), f32[16,64,768]{2,1,0:T(8,128)}, u32[]{:S(2)}, u32[]{:S(2)}) async-start(f32[16,64,768]{2,1,0:T(8,128)} %copy.164), calls=%async_computation | async-start | bytes 6291456 | tf_op jit(solution)/shard_map/all_to_all | solution.py:9
Sparse Core Ops, SparseCore 0:
  10.3 93.1 all-gather.1
